TPU v7x, 512 devices: a whole 4x8x8 slice. The times are simulated.
512 devices in a mesh: ctx: 64 (over x, z, core), head: 8 (over y).
Axes of the slice: x: 4, y: 8, z: 8, core: 2. Of those that a mesh axis runs over, the one named last changes fastest.
Arguments:
- query_rows: bfloat16 [65536, 1024], P('ctx', 'head'), may hold values from -8 to 8
- key_rows: bfloat16 [65536, 1024], P('ctx', 'head'), may hold values from -8 to 8
- value_rows: bfloat16 [65536, 1024], P('ctx', 'head'), may hold values from -6 to 6
- out_grad: bfloat16 [65536, 1024], P('ctx', 'head'), may hold values from -6 to 6
- out_weight: bfloat16 [1024, 1024], P('head'), may hold values from -0.1875 to 0.1875
- neighbours: int32 [512, 12], replicated, may hold values from 0 to 511, as said below
- counts: int32 [512], replicated, may hold values from 3 to 12, as said below
Outputs:
- query_grad: bfloat16 [65536, 1024], P('ctx', 'head')
- key_grad: bfloat16 [65536, 1024], P('ctx', 'head')
- value_grad: bfloat16 [65536, 1024], P('ctx', 'head')
- weight_grad: float32 [1024, 1024], P('head')
Inputs may be any that keep to these rules, and one draw needn't show every extreme that they name: `neighbours`: row g names block g in slot 0, then distinct blocks held by ctx indices g // 8 - 1 to g // 8 + 1; slots 1 and 2 include a block of each of the ctx indices g // 8 - 1 and g // 8 + 1 that exists; slots from counts[g] on hold g again. `counts`: block 0 uses all 12 slots.
All inputs are finite; a program needn't handle non-finite values.
Results may differ from a plain program's by a relative error of at most 0.012.
The roundings to bfloat16 on the way count: a program that leaves them out, or rounds other values in their place, can miss the bound.
Values may be sent and summed in bfloat16 or wider, within the bound.
No kernel may reach another device: no remote copies, remote signals or barrier semaphores. Data moves between devices by JAX's collectives and lax.ppermute only.
A program may use at most 64 MiB of HBM per device.

v0:
```python
import jax
import jax.numpy as jnp
from jax import lax
from jax.sharding import PartitionSpec as P

HD = 64
BS = 128


def with_halo(cells, sides, width):
    for axis, dim in sides:
        count = lax.axis_size(axis)
        ends = count - 1
        head = lax.slice_in_dim(cells, 0, width, axis=dim)
        tail = lax.slice_in_dim(cells, cells.shape[dim] - width, cells.shape[dim], axis=dim)
        cells = jnp.concatenate(
            [
                lax.ppermute(tail, axis, [(i, (i + 1) % count) for i in range(ends)]),
                cells,
                lax.ppermute(head, axis, [((i + 1) % count, i) for i in range(ends)]),
            ],
            axis=dim,
        )
    return cells


def shifted(x, axis, by):
    count = lax.axis_size(axis)
    pairs = [(i, i + by) for i in range(count) if 0 <= i + by < count]
    return lax.ppermute(x, axis, pairs)


def head_scores(query_block, key_block, factor):
    return (
        jnp.einsum("qhd,khd->hqk", query_block, key_block, preferred_element_type=jnp.float32)
        * factor
    )


def masked_scores(query_block, key_block, usable, factor):
    key_mask = jnp.repeat(usable, key_block.shape[0] // usable.shape[0])
    return jnp.where(key_mask[None, None, :], head_scores(query_block, key_block, factor), -1e30)


def padded_forward(query_block, key_block, value_block, usable, factor):
    scores = masked_scores(query_block, key_block, usable, factor)
    highest = jnp.max(scores, axis=2)
    log_total = highest + jnp.log(jnp.sum(jnp.exp(scores - highest[:, :, None]), axis=2))
    soft_weights = jnp.exp(scores - log_total[:, :, None]).astype(jnp.bfloat16)
    attended = jnp.einsum(
        "hqk,khd->qhd", soft_weights, value_block, preferred_element_type=jnp.float32
    )
    return (attended.astype(jnp.bfloat16), log_total)


def pair_backward(
    query_block, grad_block, log_total, dot_block, key_block, value_block, usable, factor
):
    scores = masked_scores(query_block, key_block, usable, factor)
    soft_full = jnp.exp(scores - log_total[:, :, None])
    grad_weights = jnp.einsum(
        "qhd,khd->hqk", grad_block, value_block, preferred_element_type=jnp.float32
    )
    grad_scores = (soft_full * (grad_weights - dot_block[:, :, None])).astype(jnp.bfloat16)
    grad_query = (
        jnp.einsum("hqk,khd->qhd", grad_scores, key_block, preferred_element_type=jnp.float32)
        * factor
    )
    grad_key = (
        jnp.einsum("hqk,qhd->khd", grad_scores, query_block, preferred_element_type=jnp.float32)
        * factor
    )
    grad_value = jnp.einsum(
        "hqk,qhd->khd",
        soft_full.astype(jnp.bfloat16),
        grad_block,
        preferred_element_type=jnp.float32,
    )
    return (grad_query, grad_key, grad_value)


def body(query_rows, key_rows, value_rows, out_grad, out_weight, neighbours, counts):
    row_count, col_count = query_rows.shape
    head_count = col_count // HD
    blocks = row_count // BS
    extent = 3 * blocks
    slot_total = neighbours.shape[1]
    block_total = counts.shape[0]
    factor = HD ** (-0.5)
    ctx_index = lax.axis_index("ctx")
    offset = (ctx_index - 1) * blocks
    packed = jnp.concatenate([key_rows, value_rows], axis=1)
    window = with_halo(packed, (("ctx", 0),), row_count)
    window = window.reshape(extent, BS, 2 * col_count)
    slot_ids = jnp.arange(slot_total, dtype=jnp.int32)
    query_blocks = query_rows.reshape(blocks, BS, head_count, HD)

    def fetch_all(places):
        picked = window[places]
        key_block = picked[:, :, :col_count].reshape(slot_total * BS, head_count, HD)
        value_block = picked[:, :, col_count:].reshape(slot_total * BS, head_count, HD)
        return (key_block, value_block)

    def slot_table(block_id):
        inside = (block_id >= 0) & (block_id < block_total)
        clamped = jnp.clip(block_id, 0, block_total - 1)
        relative = neighbours[clamped] - offset
        places = jnp.clip(relative, 0, extent - 1)
        active = jnp.where(inside, counts[clamped], 0)
        return (relative, places, active)

    def forward_block(block_index):
        relative, places, active = slot_table(ctx_index * blocks + block_index)
        query_block = query_blocks[block_index]
        key_block, value_block = fetch_all(places)
        return padded_forward(query_block, key_block, value_block, slot_ids < active, factor)

    attended_blocks, log_totals = lax.map(forward_block, jnp.arange(blocks, dtype=jnp.int32))
    attended = attended_blocks.reshape(row_count, col_count)
    shard_piece = lax.all_gather(out_grad, "head", axis=1, tiled=True)
    grad_sum = jnp.einsum("ro,jo->rj", shard_piece, out_weight, preferred_element_type=jnp.float32)
    product = jnp.einsum("rj,ro->jo", attended, shard_piece, preferred_element_type=jnp.float32)
    weight_sum = product
    grad_sum, weight_sum = (grad_sum, weight_sum)
    node_count = row_count * lax.axis_size("ctx")
    weight_grad = lax.psum(weight_sum, "ctx") * node_count ** (-0.5)
    grad_attended = grad_sum.astype(jnp.bfloat16)
    grad_blocks = grad_attended.reshape(blocks, BS, head_count, HD)
    row_dots = jnp.sum(
        grad_blocks.astype(jnp.float32) * attended_blocks.astype(jnp.float32), axis=3
    ).transpose(0, 2, 1)

    def sweep_step(totals, block_index):
        relative, places, active = slot_table(ctx_index * blocks + block_index)
        query_block = query_blocks[block_index]
        grad_block = grad_blocks[block_index]
        log_total = log_totals[block_index]
        dot_block = row_dots[block_index]
        key_block, value_block = fetch_all(places)
        grad_query, grad_key, grad_value = pair_backward(
            query_block,
            grad_block,
            log_total,
            dot_block,
            key_block,
            value_block,
            slot_ids < active,
            factor,
        )
        update = jnp.concatenate(
            [
                grad_key.reshape(slot_total, BS, col_count),
                grad_value.reshape(slot_total, BS, col_count),
            ],
            axis=2,
        )
        totals = totals.at[places].add(jnp.where((slot_ids < active)[:, None, None], update, 0.0))
        return (totals, grad_query.astype(jnp.bfloat16))

    blank_totals = jnp.zeros((extent, BS, 2 * col_count), jnp.float32)
    totals, grad_queries = lax.scan(sweep_step, blank_totals, jnp.arange(blocks, dtype=jnp.int32))
    middle = totals[blocks : 2 * blocks]
    from_right = shifted(totals[:blocks], "ctx", -1)
    from_left = shifted(totals[2 * blocks :], "ctx", 1)
    combined = middle + from_right + from_left
    query_grad = grad_queries.reshape(row_count, col_count)
    key_grad = combined[:, :, :col_count].reshape(row_count, col_count).astype(jnp.bfloat16)
    value_grad = combined[:, :, col_count:].reshape(row_count, col_count).astype(jnp.bfloat16)
    return (query_grad, key_grad, value_grad, weight_grad)


def solution(mesh):
    placed = (
        P("ctx", "head"),
        P("ctx", "head"),
        P("ctx", "head"),
        P("ctx", "head"),
        P("head", None),
        P(),
        P(),
    )
    return jax.shard_map(
        body,
        mesh=mesh,
        in_specs=placed,
        out_specs=(P("ctx", "head"), P("ctx", "head"), P("ctx", "head"), P("head", None)),
        check_vma=False,
    )
```

profile of v0, /device:TPU:8, one launch (start us, length us, event | category | flops | bytes accessed | tf_op | source)
XLA Modules:
  0.0 513.1 jit_solution(8677155265565717120)
XLA Ops:
  9.3 1.3 collective-permute-start.1
  10.6 3.8 collective-permute-start
  14.6 1.6 copy.63
  18.2 1.3 pad_maximum_fusion
  20.3 81.6 %while.30 = (s32[]{:T(128)}, bf16[8,128,2,64]{1,3,2,0:T(8,128)(2,1)}, f32[8,2,128]{2,1,0:T(2,128)S(1)}, s32[8]{0:T(128)S(1)}, s32[]{:T(128)}, /*index=5*/s32[512...) while((s32[]{:T(128)}, ...), condition=%wide.region_3.4_spmd.clone, body=%wide.region_0.3_spmd.clone.sunk | while | flops 103433040 | bytes 11877893 | solution.py:118
  27.7 1.3 fusion.85
  37.9 1.3 fusion.85
  48.1 1.3 fusion.85
  58.3 1.3 fusion.85
  68.5 1.3 fusion.85
  78.7 1.3 fusion.85
  88.9 1.3 fusion.85
  99.1 1.3 fusion.85
  101.9 2.3 convolution_convert_fusion.1
  106.1 2.0 broadcast_in_dim.88
  108.1 176.7 %while.31 = (s32[]{:T(128)}, f32[24,128,256]{2,1,0:T(8,128)}, bf16[8,128,2,64]{1,3,2,0:T(8,128)(2,1)}, s32[8]{0:T(128)S(1)}, s32[]{:T(128)}, /*index=5*/s32[512,...) while((s32[]{:T(128)}, f32[24,128,256]{2,1,0:T(8,128)}, ...), condition=%wide.region_7.8_spmd.clone, body=%wide.region_5.7_spmd.clone.sunk | while | flops 255820880 | bytes 43038368 | solution.py:161
  122.4 1.4 maximum_select_fusion.2
  123.9 1.7 copy.91
  125.6 4.7 scatter_fusion
  144.6 1.4 maximum_select_fusion.2
  146.0 1.7 copy.91
  147.7 4.5 scatter_fusion
  166.6 1.4 maximum_select_fusion.2
  168.1 1.7 copy.91
  169.8 4.8 scatter_fusion
  188.9 1.4 maximum_select_fusion.2
  190.3 1.7 copy.91
  192.0 4.5 scatter_fusion
  210.8 1.4 maximum_select_fusion.2
  212.3 1.7 copy.91
  214.0 4.5 scatter_fusion
  226.0 1.3 fusion.100
  232.8 1.4 maximum_select_fusion.2
  234.2 1.7 copy.91
  235.9 4.8 scatter_fusion
  255.0 1.4 maximum_select_fusion.2
  256.5 1.7 copy.91
  258.2 4.4 scatter_fusion
  277.0 1.4 maximum_select_fusion.2
  278.4 1.7 copy.91
  280.1 4.7 scatter_fusion
  284.8 3.2 fusion.46
  288.1 1.3 collective-permute-start.2
  289.4 5.9 %collective-permute-start.3 = (f32[8,128,256]{2,1,0:T(8,128)}, f32[8,128,256]{2,1,0:T(8,128)S(1)}, u32[]{:S(2)}, u32[]{:S(2)}) collective-permute-start(f32[8,128,256]{2,1,0:T(8,128)} %get-tuple-element.506), channel_id=1, source_target_pairs={{0,8},{8,16},{16,24},{24,32},{32,40},{40,48},{48,56},{56,64},{64,7... | collective-permute-start | bytes 3145736 | tf_op jit(solution)/shard_map/ppermute | solution.py:30
  296.7 1.3 copy.70
  298.9 203.1 %all-reduce.2.cloned.1.call-done = f32[128,1024]{1,0:T(8,128)} async-done(((f32[128,1024]{1,0:T(8,128)}), f32[128,1024]{1,0:T(8,128)}) %all-reduce.2.cloned.1.call-update) | async-done | bytes 524304 | tf_op jit(solution)/shard_map/psum | solution.py:126
  502.0 1.9 broadcast_multiply_fusion
  503.9 1.4 add_convert_fusion
  (359 shorter events, 142.3 us)
Async XLA Ops:
  7.2 94.7 %copy-start = (bf16[128,1024]{1,0:T(8,128)(2,1)S(1)}, bf16[128,1024]{1,0:T(8,128)(2,1)}, u32[]{:S(2)}) copy-start(bf16[128,1024]{1,0:T(8,128)(2,1)} %param.15) | copy-start | bytes 786436
  7.2 9.0 %copy-start.7 = (bf16[1024,128]{1,0:T(8,128)(2,1)S(1)}, bf16[1024,128]{1,0:T(8,128)(2,1)}, u32[]{:S(2)}) copy-start(bf16[1024,128]{1,0:T(8,128)(2,1)} %param.11) | copy-start | bytes 786436
  7.2 94.7 %all-gather.2.cloned.1.call-start = ((), (), s32[]{:S(2)}) async-start(), calls=%async_computation | async-start | bytes 2359296 | tf_op jit(solution)/shard_map/all_gather | solution.py:120
  9.3 8.1 %collective-permute-start.1 = (bf16[1024,256]{1,0:T(8,128)(2,1)S(1)}, bf16[1024,256]{1,0:T(8,128)(2,1)S(1)}, u32[]{:S(2)}, u32[]{:S(2)}) collective-permute-start(bf16[1024,256]{1,0:T(8,128)(2,1)S(1)} %constant_dynamic-update-slice_fusion), channel_id=1, source_target_pairs={{8,0},{16,8},{24,16},{32,24},{40,32},{48,40},{56,48},{64,56},{72,6... | collective-permute-start | bytes 1572872 | tf_op jit(solution)/shard_map/ppermute | solution.py:20
  10.6 7.6 %collective-permute-start = (bf16[1024,256]{1,0:T(8,128)(2,1)S(1)}, bf16[1024,256]{1,0:T(8,128)(2,1)}, u32[]{:S(2)}, u32[]{:S(2)}) collective-permute-start(bf16[1024,256]{1,0:T(8,128)(2,1)S(1)} %constant_dynamic-update-slice_fusion), channel_id=1, source_target_pairs={{0,8},{8,16},{16,24},{24,32},{32,40},{40,48},{48,56},{56,64},{64,7... | collective-permute-start | bytes 1572872 | tf_op jit(solution)/shard_map/ppermute | solution.py:18
  14.5 487.5 %all-reduce.2.cloned.1.call-start = ((), (), s32[]{:S(2)}) async-start(), calls=%async_computation.1 | async-start | bytes 1048576 | tf_op jit(solution)/shard_map/psum | solution.py:126
  17.4 2.9 copy-start.8
  17.4 0.8 copy-start.6
  101.9 3.3 copy-start.4
  108.1 6.1 %copy-start.1 = (bf16[24,128,256]{2,1,0:T(8,128)(2,1)}, bf16[24,128,256]{2,1,0:T(8,128)(2,1)S(1)}, u32[]{:S(2)}) copy-start(bf16[24,128,256]{2,1,0:T(8,128)(2,1)S(1)} %get-tuple-element.755) | copy-start | bytes 4718596 | tf_op jit(solution)/shard_map/while
  125.6 4.7 copy-start.2
  130.3 6.1 %copy-start.1 = (bf16[24,128,256]{2,1,0:T(8,128)(2,1)}, bf16[24,128,256]{2,1,0:T(8,128)(2,1)S(1)}, u32[]{:S(2)}) copy-start(bf16[24,128,256]{2,1,0:T(8,128)(2,1)S(1)} %get-tuple-element.755) | copy-start | bytes 4718596 | tf_op jit(solution)/shard_map/while
  147.7 4.5 copy-start.2
  152.3 6.1 %copy-start.1 = (bf16[24,128,256]{2,1,0:T(8,128)(2,1)}, bf16[24,128,256]{2,1,0:T(8,128)(2,1)S(1)}, u32[]{:S(2)}) copy-start(bf16[24,128,256]{2,1,0:T(8,128)(2,1)S(1)} %get-tuple-element.755) | copy-start | bytes 4718596 | tf_op jit(solution)/shard_map/while
  169.8 4.8 copy-start.2
  174.5 6.1 %copy-start.1 = (bf16[24,128,256]{2,1,0:T(8,128)(2,1)}, bf16[24,128,256]{2,1,0:T(8,128)(2,1)S(1)}, u32[]{:S(2)}) copy-start(bf16[24,128,256]{2,1,0:T(8,128)(2,1)S(1)} %get-tuple-element.755) | copy-start | bytes 4718596 | tf_op jit(solution)/shard_map/while
  192.0 4.5 copy-start.2
  196.5 6.1 %copy-start.1 = (bf16[24,128,256]{2,1,0:T(8,128)(2,1)}, bf16[24,128,256]{2,1,0:T(8,128)(2,1)S(1)}, u32[]{:S(2)}) copy-start(bf16[24,128,256]{2,1,0:T(8,128)(2,1)S(1)} %get-tuple-element.755) | copy-start | bytes 4718596 | tf_op jit(solution)/shard_map/while
  214.0 4.5 copy-start.2
  218.4 6.1 %copy-start.1 = (bf16[24,128,256]{2,1,0:T(8,128)(2,1)}, bf16[24,128,256]{2,1,0:T(8,128)(2,1)S(1)}, u32[]{:S(2)}) copy-start(bf16[24,128,256]{2,1,0:T(8,128)(2,1)S(1)} %get-tuple-element.755) | copy-start | bytes 4718596 | tf_op jit(solution)/shard_map/while
  235.9 4.8 copy-start.2
  240.7 6.1 %copy-start.1 = (bf16[24,128,256]{2,1,0:T(8,128)(2,1)}, bf16[24,128,256]{2,1,0:T(8,128)(2,1)S(1)}, u32[]{:S(2)}) copy-start(bf16[24,128,256]{2,1,0:T(8,128)(2,1)S(1)} %get-tuple-element.755) | copy-start | bytes 4718596 | tf_op jit(solution)/shard_map/while
  258.2 4.4 copy-start.2
  262.6 6.1 %copy-start.1 = (bf16[24,128,256]{2,1,0:T(8,128)(2,1)}, bf16[24,128,256]{2,1,0:T(8,128)(2,1)S(1)}, u32[]{:S(2)}) copy-start(bf16[24,128,256]{2,1,0:T(8,128)(2,1)S(1)} %get-tuple-element.755) | copy-start | bytes 4718596 | tf_op jit(solution)/shard_map/while
  280.1 4.7 copy-start.2
  284.8 10.4 %copy-start.5 = (bf16[8,128,2,64]{1,3,2,0:T(8,128)(2,1)S(1)}, bf16[8,128,2,64]{1,3,2,0:T(8,128)(2,1)}, u32[]{:S(2)}) copy-start(bf16[8,128,2,64]{1,3,2,0:T(8,128)(2,1)} %get-tuple-element.294) | copy-start | bytes 786436
  284.8 10.6 %copy-start.3 = (bf16[1024,1024]{1,0:T(8,128)(2,1)S(1)}, bf16[1024,1024]{1,0:T(8,128)(2,1)}, u32[]{:S(2)}) copy-start(bf16[1024,1024]{1,0:T(8,128)(2,1)} %all-gather.2.cloned.1.call-done) | copy-start | bytes 6291460
  288.1 215.8 %collective-permute-start.2 = (f32[8,128,256]{2,1,0:T(8,128)}, f32[8,128,256]{2,1,0:T(8,128)S(1)}, u32[]{:S(2)}, u32[]{:S(2)}) collective-permute-start(f32[8,128,256]{2,1,0:T(8,128)} %get-tuple-element.505), channel_id=1, source_target_pairs={{8,0},{16,8},{24,16},{32,24},{40,32},{48,40},{56,48},{64,56},{72,6... | collective-permute-start | bytes 3145736 | tf_op jit(solution)/shard_map/ppermute | solution.py:30
  289.4 214.6 %collective-permute-start.3 = (f32[8,128,256]{2,1,0:T(8,128)}, f32[8,128,256]{2,1,0:T(8,128)S(1)}, u32[]{:S(2)}, u32[]{:S(2)}) collective-permute-start(f32[8,128,256]{2,1,0:T(8,128)} %get-tuple-element.506), channel_id=1, source_target_pairs={{0,8},{8,16},{16,24},{24,32},{32,40},{40,48},{48,56},{56,64},{64,7... | collective-permute-start | bytes 3145736 | tf_op jit(solution)/shard_map/ppermute | solution.py:30
Sparse Core Ops, SparseCore 0:
  14.6 56.4 all-gather.1
  296.8 205.1 all-reduce.1
where the time goes:
time: 518 us; the launch traced here: 513 us
  waiting for transfers between devices  203 us (39%)
  local copies, waits for them, and re-layouts  96.8 us (19%)
  other arithmetic  67.7 us (13%)
  matrix products  66.1 us (13%)
  loops' own time  52.9 us (10%)
  between operations  14.2 us (3%)
  starting transfers between devices  12.4 us (2%)
    psum x1, waiting for transfers between devices, body(): weight_grad = lax.psum(weight_sum, 'ctx') * node_count ** (-0.5)  203 us
    scatter-add x8, other arithmetic, sweep_step(): totals.at[places]  36.9 us
    another operation x1, loops' own time, body(): lax.map(forward_block, jnp.arange(blocks, dtype=jnp.int32))  26.5 us
    another operation x1, loops' own time, body(): lax.scan(sweep_step, blank_totals, jnp.arange(blocks, dtype=jnp.int32))  26.4 us
    dot_general x16, matrix products, head_scores(): jnp.einsum('qhd,khd->hqk', query_block, key_block, preferred_element_type...  20.1 us
    select_n x8, local copies, waits for them, and re-layouts, sweep_step(): jnp.where((slot_ids < active)[:, None, None], update, 0.0)  13.6 us
    select_n x8, other arithmetic, sweep_step(): jnp.where((slot_ids < active)[:, None, None], update, 0.0)  11.5 us
  transfers between devices with their start and end apart: 6, of which 1 were waited for; matrix products, arithmetic and copies ran while one was open for 13% of the time, Pallas kernels for 0%

commit v1 on v0

--- a/solution.py
+++ b/solution.py
@@ -123,7 +123,7 @@
     weight_sum = product
     grad_sum, weight_sum = (grad_sum, weight_sum)
     node_count = row_count * lax.axis_size("ctx")
-    weight_grad = lax.psum(weight_sum, "ctx") * node_count ** (-0.5)
+    weight_grad = jnp.sum(lax.all_gather(weight_sum, "ctx"), axis=0) * node_count ** (-0.5)
     grad_attended = grad_sum.astype(jnp.bfloat16)
     grad_blocks = grad_attended.reshape(blocks, BS, head_count, HD)
     row_dots = jnp.sum(

time: 518 us -> 416 us (0.80)
  the two profiles are of different devices: /device:TPU:8 before, /device:TPU:46 now
where the time goes in v1:
time: 416 us; the launch traced here: 411 us
  local copies, waits for them, and re-layouts  150 us (36%)
  other arithmetic  81.2 us (20%)
  matrix products  73 us (18%)
  loops' own time  53.3 us (13%)
  starting transfers between devices  20 us (5%)
  waiting for transfers between devices  18.7 us (4%)
  between operations  14.2 us (3%)
    scatter-add x8, other arithmetic, sweep_step(): totals.at[places]  36.9 us
    slice x24, local copies, waits for them, and re-layouts, fetch_all(): picked[:, :, col_count:].reshape(slot_total * BS, head_count, HD)  28.8 us
    another operation x1, loops' own time, body(): lax.scan(sweep_step, blank_totals, jnp.arange(blocks, dtype=jnp.int32))  27.2 us
    another operation x1, loops' own time, body(): lax.map(forward_block, jnp.arange(blocks, dtype=jnp.int32))  26.1 us
    dot_general x16, matrix products, head_scores(): jnp.einsum('qhd,khd->hqk', query_block, key_block, preferred_element_type...  22.5 us
    reshape x16, local copies, waits for them, and re-layouts, fetch_all(): picked[:, :, col_count:].reshape(slot_total * BS, head_count, HD)  18.6 us
    dot_general x8, matrix products, padded_forward(): jnp.einsum('hqk,khd->qhd', soft_weights, value_block, preferred_element_t...  16.6 us
    ppermute x2, waiting for transfers between devices, shifted(): return lax.ppermute(x, axis, pairs)  15.1 us
  transfers between devices with their start and end apart: 6, of which 4 were waited for; matrix products, arithmetic and copies ran while one was open for 70% of the time, Pallas kernels for 0%

profile of v1, /device:TPU:46, one launch (start us, length us, event | category | flops | bytes accessed | tf_op | source)
XLA Modules:
  0.0 410.7 jit_solution(6168499971818952287)
XLA Ops:
  9.3 1.9 collective-permute-start
  11.2 10.7 %collective-permute-start.1 = (bf16[1024,256]{1,0:T(8,128)(2,1)S(1)}, bf16[1024,256]{1,0:T(8,128)(2,1)}, u32[]{:S(2)}, u32[]{:S(2)}) collective-permute-start(bf16[1024,256]{1,0:T(8,128)(2,1)S(1)} %constant_dynamic-update-slice_fusion), channel_id=1, source_target_pairs={{8,0},{16,8},{24,16},{32,24},{40,32},{48,40},{56,48},{64,56},{72,6... | collective-permute-start | bytes 1572872 | tf_op jit(solution)/shard_map/ppermute | solution.py:20
  30.5 131.9 %while.30 = (s32[]{:T(128)}, bf16[8,128,2,64]{1,3,2,0:T(8,128)(2,1)}, f32[8,2,128]{2,1,0:T(2,128)S(1)}, s32[8]{0:T(128)S(1)}, s32[]{:T(128)}, /*index=5*/s32[512...) while((s32[]{:T(128)}, ...), condition=%wide.region_3.4_spmd.clone, body=%wide.region_0.3_spmd.clone.sunk | while | flops 103433040 | bytes 11878393 | solution.py:118
  40.6 2.2 copy.87
  42.8 2.1 reshape.214
  44.9 2.1 fusion.86
  57.1 2.2 copy.87
  59.3 2.1 reshape.214
  61.4 2.1 fusion.86
  73.6 2.2 copy.87
  75.8 2.1 reshape.214
  77.9 2.1 fusion.86
  90.1 2.2 copy.87
  92.3 2.1 reshape.214
  94.4 2.1 fusion.86
  106.6 2.2 copy.87
  108.8 2.1 reshape.214
  110.9 2.1 fusion.86
  123.1 2.2 copy.87
  125.3 2.1 reshape.214
  127.3 2.1 fusion.86
  139.6 2.2 copy.87
  141.8 2.1 reshape.214
  143.8 2.1 fusion.86
  156.1 2.2 copy.87
  158.3 2.1 reshape.214
  160.3 2.1 fusion.86
  163.5 2.8 fusion.40
  166.4 2.3 convolution_convert_fusion.1
  169.9 2.0 broadcast_in_dim.88
  171.9 190.0 %while.31 = (s32[]{:T(128)}, f32[24,128,256]{2,1,0:T(8,128)}, bf16[8,128,2,64]{1,3,2,0:T(8,128)(2,1)S(1)}, s32[8]{0:T(128)S(1)}, s32[]{:T(128)}, /*index=5*/s32[...) while((s32[]{:T(128)}, f32[24,128,256]{2,1,0:T(8,128)}, ...), condition=%wide.region_7.8_spmd.clone, body=%wide.region_5.7_spmd.clone.sunk | while | flops 255820880 | bytes 47757036 | solution.py:161
  190.6 4.6 %scatter_fusion = f32[24,128,256]{2,1,0:T(8,128)} fusion(f32[24,128,256]{2,1,0:T(8,128)} %get-tuple-element.729, s32[12]{0:T(128)S(1)} %fusion.97, f32[12,128,256]{2,1,0:T(8,128)} %copy.91), kind=kCustom, calls=%fused_computation.2.clone.clone.1 | custom fusion | flops 393216 | bytes 4718640 | tf_op jit(solution)/shard_map/while/body/eval_jaxpr/scatter-add | solution.py:157
  214.3 4.4 %scatter_fusion = f32[24,128,256]{2,1,0:T(8,128)} fusion(f32[24,128,256]{2,1,0:T(8,128)} %get-tuple-element.729, s32[12]{0:T(128)S(1)} %fusion.97, f32[12,128,256]{2,1,0:T(8,128)} %copy.91), kind=kCustom, calls=%fused_computation.2.clone.clone.1 | custom fusion | flops 393216 | bytes 4718640 | tf_op jit(solution)/shard_map/while/body/eval_jaxpr/scatter-add | solution.py:157
  234.4 1.9 maximum_select_fusion.2
  238.0 4.7 %scatter_fusion = f32[24,128,256]{2,1,0:T(8,128)} fusion(f32[24,128,256]{2,1,0:T(8,128)} %get-tuple-element.729, s32[12]{0:T(128)S(1)} %fusion.97, f32[12,128,256]{2,1,0:T(8,128)} %copy.91), kind=kCustom, calls=%fused_computation.2.clone.clone.1 | custom fusion | flops 393216 | bytes 4718640 | tf_op jit(solution)/shard_map/while/body/eval_jaxpr/scatter-add | solution.py:157
  258.4 1.8 maximum_select_fusion.2
  261.9 4.8 %scatter_fusion = f32[24,128,256]{2,1,0:T(8,128)} fusion(f32[24,128,256]{2,1,0:T(8,128)} %get-tuple-element.729, s32[12]{0:T(128)S(1)} %fusion.97, f32[12,128,256]{2,1,0:T(8,128)} %copy.91), kind=kCustom, calls=%fused_computation.2.clone.clone.1 | custom fusion | flops 393216 | bytes 4718640 | tf_op jit(solution)/shard_map/while/body/eval_jaxpr/scatter-add | solution.py:157
  282.3 1.9 maximum_select_fusion.2
  285.9 4.5 %scatter_fusion = f32[24,128,256]{2,1,0:T(8,128)} fusion(f32[24,128,256]{2,1,0:T(8,128)} %get-tuple-element.729, s32[12]{0:T(128)S(1)} %fusion.97, f32[12,128,256]{2,1,0:T(8,128)} %copy.91), kind=kCustom, calls=%fused_computation.2.clone.clone.1 | custom fusion | flops 393216 | bytes 4718640 | tf_op jit(solution)/shard_map/while/body/eval_jaxpr/scatter-add | solution.py:157
  309.5 4.8 %scatter_fusion = f32[24,128,256]{2,1,0:T(8,128)} fusion(f32[24,128,256]{2,1,0:T(8,128)} %get-tuple-element.729, s32[12]{0:T(128)S(1)} %fusion.97, f32[12,128,256]{2,1,0:T(8,128)} %copy.91), kind=kCustom, calls=%fused_computation.2.clone.clone.1 | custom fusion | flops 393216 | bytes 4718640 | tf_op jit(solution)/shard_map/while/body/eval_jaxpr/scatter-add | solution.py:157
  333.4 4.4 %scatter_fusion = f32[24,128,256]{2,1,0:T(8,128)} fusion(f32[24,128,256]{2,1,0:T(8,128)} %get-tuple-element.729, s32[12]{0:T(128)S(1)} %fusion.97, f32[12,128,256]{2,1,0:T(8,128)} %copy.91), kind=kCustom, calls=%fused_computation.2.clone.clone.1 | custom fusion | flops 393216 | bytes 4718640 | tf_op jit(solution)/shard_map/while/body/eval_jaxpr/scatter-add | solution.py:157
  356.9 4.7 %scatter_fusion = f32[24,128,256]{2,1,0:T(8,128)} fusion(f32[24,128,256]{2,1,0:T(8,128)} %get-tuple-element.729, s32[12]{0:T(128)S(1)} %fusion.97, f32[12,128,256]{2,1,0:T(8,128)} %copy.91), kind=kCustom, calls=%fused_computation.2.clone.clone.1 | custom fusion | flops 393216 | bytes 4718640 | tf_op jit(solution)/shard_map/while/body/eval_jaxpr/scatter-add | solution.py:157
  362.0 3.1 fusion.46
  365.0 5.4 %collective-permute-start.2 = (f32[8,128,256]{2,1,0:T(8,128)}, f32[8,128,256]{2,1,0:T(8,128)S(1)}, u32[]{:S(2)}, u32[]{:S(2)}) collective-permute-start(f32[8,128,256]{2,1,0:T(8,128)} %get-tuple-element.505), channel_id=1, source_target_pairs={{8,0},{16,8},{24,16},{32,24},{40,32},{48,40},{56,48},{64,56},{72,6... | collective-permute-start | bytes 3145736 | tf_op jit(solution)/shard_map/ppermute | solution.py:30
  370.5 1.9 collective-permute-start.3
  373.7 9.3 %collective-permute-done.2 = f32[8,128,256]{2,1,0:T(8,128)S(1)} collective-permute-done((f32[8,128,256]{2,1,0:T(8,128)}, f32[8,128,256]{2,1,0:T(8,128)S(1)}, u32[]{:S(2)}, u32[]{:S(2)}) %collective-permute-start.2) | collective-permute-done | bytes 1048608 | tf_op jit(solution)/shard_map/ppermute | solution.py:30
  383.1 5.8 %collective-permute-done.3 = f32[8,128,256]{2,1,0:T(8,128)S(1)} collective-permute-done((f32[8,128,256]{2,1,0:T(8,128)}, f32[8,128,256]{2,1,0:T(8,128)S(1)}, u32[]{:S(2)}, u32[]{:S(2)}) %collective-permute-start.3) | collective-permute-done | bytes 1048608 | tf_op jit(solution)/shard_map/ppermute | solution.py:30
  391.2 11.8 %reduce_sum.30 = f32[128,1024]{1,0:T(8,128)S(1)} reduce(f32[64,128,1024]{2,1,0:T(8,128)} %bitcast.152, f32[]{:T(128)} %constant.121.clone.1), dimensions={0}, to_apply=%region_8.9 | reduce | flops 8257536 | bytes 34078724 | tf_op jit(solution)/shard_map/reduce_sum | solution.py:126
  (404 shorter events, 193.1 us)
Async XLA Ops:
  7.2 159.2 %copy-start = (bf16[128,1024]{1,0:T(8,128)(2,1)S(1)}, bf16[128,1024]{1,0:T(8,128)(2,1)}, u32[]{:S(2)}) copy-start(bf16[128,1024]{1,0:T(8,128)(2,1)} %param.15) | copy-start | bytes 786436
  7.2 17.0 %copy-start.8 = (s32[512,12]{0,1:T(8,128)S(1)}, s32[512,12]{0,1:T(8,128)}, u32[]{:S(2)}) copy-start(s32[512,12]{0,1:T(8,128)} %param.16) | copy-start | bytes 73732
  7.2 156.3 %all-gather.4.cloned.1.call-start = ((), (), s32[]{:S(2)}) async-start(), calls=%async_computation | async-start | bytes 2359296 | tf_op jit(solution)/shard_map/all_gather | solution.py:120
  9.3 17.5 %collective-permute-start = (bf16[1024,256]{1,0:T(8,128)(2,1)S(1)}, bf16[1024,256]{1,0:T(8,128)(2,1)S(1)}, u32[]{:S(2)}, u32[]{:S(2)}) collective-permute-start(bf16[1024,256]{1,0:T(8,128)(2,1)S(1)} %constant_dynamic-update-slice_fusion), channel_id=1, source_target_pairs={{0,8},{8,16},{16,24},{24,32},{32,40},{40,48},{48,56},{56,64},{64,7... | collective-permute-start | bytes 1572872 | tf_op jit(solution)/shard_map/ppermute | solution.py:18
  11.2 17.3 %collective-permute-start.1 = (bf16[1024,256]{1,0:T(8,128)(2,1)S(1)}, bf16[1024,256]{1,0:T(8,128)(2,1)}, u32[]{:S(2)}, u32[]{:S(2)}) collective-permute-start(bf16[1024,256]{1,0:T(8,128)(2,1)S(1)} %constant_dynamic-update-slice_fusion), channel_id=1, source_target_pairs={{8,0},{16,8},{24,16},{32,24},{40,32},{48,40},{56,48},{64,56},{72,6... | collective-permute-start | bytes 1572872 | tf_op jit(solution)/shard_map/ppermute | solution.py:20
  21.9 369.3 %all-gather.6.cloned.1.call-start = ((), (), s32[]{:S(2)}) async-start(), calls=%async_computation.1 | async-start | bytes 34078720 | tf_op jit(solution)/shard_map/all_gather | solution.py:126
  25.0 5.5 %copy-start.9 = (s32[512]{0:T(512)S(1)}, s32[512]{0:T(512)}, u32[]{:S(2)}) copy-start(s32[512]{0:T(512)} %param.17) | copy-start | bytes 6148
  166.4 3.3 copy-start.7
  171.9 6.9 %copy-start.2 = (bf16[24,128,256]{2,1,0:T(8,128)(2,1)}, bf16[24,128,256]{2,1,0:T(8,128)(2,1)S(1)}, u32[]{:S(2)}) copy-start(bf16[24,128,256]{2,1,0:T(8,128)(2,1)S(1)} %get-tuple-element.755) | copy-start | bytes 4718596 | tf_op jit(solution)/shard_map/while
  179.3 1.6 copy-start.6
  179.6 2.1 copy-start.4
  190.6 4.6 %copy-start.5 = (bf16[1536,2,64]{0,2,1:T(8,128)(2,1)S(1)}, bf16[1536,2,64]{0,2,1:T(8,128)(2,1)}, u32[]{:S(2)}) copy-start(bf16[1536,2,64]{0,2,1:T(8,128)(2,1)} %copy-done.4) | copy-start | bytes 1179652 | tf_op jit(solution)/shard_map/while
  190.6 5.0 %copy-start.3 = (bf16[24,128,256]{2,1,0:T(8,128)(2,1)S(1)}, bf16[24,128,256]{2,1,0:T(8,128)(2,1)}, u32[]{:S(2)}) copy-start(bf16[24,128,256]{2,1,0:T(8,128)(2,1)} %copy-done.2) | copy-start | bytes 4718596 | tf_op jit(solution)/shard_map/while
  195.7 6.9 %copy-start.2 = (bf16[24,128,256]{2,1,0:T(8,128)(2,1)}, bf16[24,128,256]{2,1,0:T(8,128)(2,1)S(1)}, u32[]{:S(2)}) copy-start(bf16[24,128,256]{2,1,0:T(8,128)(2,1)S(1)} %get-tuple-element.755) | copy-start | bytes 4718596 | tf_op jit(solution)/shard_map/while
  203.0 1.6 copy-start.6
  203.3 2.1 copy-start.4
  214.3 4.4 %copy-start.5 = (bf16[1536,2,64]{0,2,1:T(8,128)(2,1)S(1)}, bf16[1536,2,64]{0,2,1:T(8,128)(2,1)}, u32[]{:S(2)}) copy-start(bf16[1536,2,64]{0,2,1:T(8,128)(2,1)} %copy-done.4) | copy-start | bytes 1179652 | tf_op jit(solution)/shard_map/while
  214.3 4.8 %copy-start.3 = (bf16[24,128,256]{2,1,0:T(8,128)(2,1)S(1)}, bf16[24,128,256]{2,1,0:T(8,128)(2,1)}, u32[]{:S(2)}) copy-start(bf16[24,128,256]{2,1,0:T(8,128)(2,1)} %copy-done.2) | copy-start | bytes 4718596 | tf_op jit(solution)/shard_map/while
  219.2 6.9 %copy-start.2 = (bf16[24,128,256]{2,1,0:T(8,128)(2,1)}, bf16[24,128,256]{2,1,0:T(8,128)(2,1)S(1)}, u32[]{:S(2)}) copy-start(bf16[24,128,256]{2,1,0:T(8,128)(2,1)S(1)} %get-tuple-element.755) | copy-start | bytes 4718596 | tf_op jit(solution)/shard_map/while
  226.8 2.1 copy-start.4
  238.0 4.7 %copy-start.5 = (bf16[1536,2,64]{0,2,1:T(8,128)(2,1)S(1)}, bf16[1536,2,64]{0,2,1:T(8,128)(2,1)}, u32[]{:S(2)}) copy-start(bf16[1536,2,64]{0,2,1:T(8,128)(2,1)} %copy-done.4) | copy-start | bytes 1179652 | tf_op jit(solution)/shard_map/while
  238.0 5.1 %copy-start.3 = (bf16[24,128,256]{2,1,0:T(8,128)(2,1)S(1)}, bf16[24,128,256]{2,1,0:T(8,128)(2,1)}, u32[]{:S(2)}) copy-start(bf16[24,128,256]{2,1,0:T(8,128)(2,1)} %copy-done.2) | copy-start | bytes 4718596 | tf_op jit(solution)/shard_map/while
  243.1 7.0 %copy-start.2 = (bf16[24,128,256]{2,1,0:T(8,128)(2,1)}, bf16[24,128,256]{2,1,0:T(8,128)(2,1)S(1)}, u32[]{:S(2)}) copy-start(bf16[24,128,256]{2,1,0:T(8,128)(2,1)S(1)} %get-tuple-element.755) | copy-start | bytes 4718596 | tf_op jit(solution)/shard_map/while
  250.5 1.6 copy-start.6
  250.8 2.1 copy-start.4
  261.9 4.8 %copy-start.5 = (bf16[1536,2,64]{0,2,1:T(8,128)(2,1)S(1)}, bf16[1536,2,64]{0,2,1:T(8,128)(2,1)}, u32[]{:S(2)}) copy-start(bf16[1536,2,64]{0,2,1:T(8,128)(2,1)} %copy-done.4) | copy-start | bytes 1179652 | tf_op jit(solution)/shard_map/while
  261.9 5.2 %copy-start.3 = (bf16[24,128,256]{2,1,0:T(8,128)(2,1)S(1)}, bf16[24,128,256]{2,1,0:T(8,128)(2,1)}, u32[]{:S(2)}) copy-start(bf16[24,128,256]{2,1,0:T(8,128)(2,1)} %copy-done.2) | copy-start | bytes 4718596 | tf_op jit(solution)/shard_map/while
  267.1 6.9 %copy-start.2 = (bf16[24,128,256]{2,1,0:T(8,128)(2,1)}, bf16[24,128,256]{2,1,0:T(8,128)(2,1)S(1)}, u32[]{:S(2)}) copy-start(bf16[24,128,256]{2,1,0:T(8,128)(2,1)S(1)} %get-tuple-element.755) | copy-start | bytes 4718596 | tf_op jit(solution)/shard_map/while
  274.4 1.6 copy-start.6
  274.7 2.1 copy-start.4
  285.9 4.5 %copy-start.5 = (bf16[1536,2,64]{0,2,1:T(8,128)(2,1)S(1)}, bf16[1536,2,64]{0,2,1:T(8,128)(2,1)}, u32[]{:S(2)}) copy-start(bf16[1536,2,64]{0,2,1:T(8,128)(2,1)} %copy-done.4) | copy-start | bytes 1179652 | tf_op jit(solution)/shard_map/while
  285.9 4.9 %copy-start.3 = (bf16[24,128,256]{2,1,0:T(8,128)(2,1)S(1)}, bf16[24,128,256]{2,1,0:T(8,128)(2,1)}, u32[]{:S(2)}) copy-start(bf16[24,128,256]{2,1,0:T(8,128)(2,1)} %copy-done.2) | copy-start | bytes 4718596 | tf_op jit(solution)/shard_map/while
  290.8 6.9 %copy-start.2 = (bf16[24,128,256]{2,1,0:T(8,128)(2,1)}, bf16[24,128,256]{2,1,0:T(8,128)(2,1)S(1)}, u32[]{:S(2)}) copy-start(bf16[24,128,256]{2,1,0:T(8,128)(2,1)S(1)} %get-tuple-element.755) | copy-start | bytes 4718596 | tf_op jit(solution)/shard_map/while
  298.2 1.6 copy-start.6
  298.5 2.1 copy-start.4
  309.5 4.8 %copy-start.5 = (bf16[1536,2,64]{0,2,1:T(8,128)(2,1)S(1)}, bf16[1536,2,64]{0,2,1:T(8,128)(2,1)}, u32[]{:S(2)}) copy-start(bf16[1536,2,64]{0,2,1:T(8,128)(2,1)} %copy-done.4) | copy-start | bytes 1179652 | tf_op jit(solution)/shard_map/while
  309.5 5.2 %copy-start.3 = (bf16[24,128,256]{2,1,0:T(8,128)(2,1)S(1)}, bf16[24,128,256]{2,1,0:T(8,128)(2,1)}, u32[]{:S(2)}) copy-start(bf16[24,128,256]{2,1,0:T(8,128)(2,1)} %copy-done.2) | copy-start | bytes 4718596 | tf_op jit(solution)/shard_map/while
  314.7 6.9 %copy-start.2 = (bf16[24,128,256]{2,1,0:T(8,128)(2,1)}, bf16[24,128,256]{2,1,0:T(8,128)(2,1)S(1)}, u32[]{:S(2)}) copy-start(bf16[24,128,256]{2,1,0:T(8,128)(2,1)S(1)} %get-tuple-element.755) | copy-start | bytes 4718596 | tf_op jit(solution)/shard_map/while
  322.4 2.1 copy-start.4
  333.4 4.4 %copy-start.5 = (bf16[1536,2,64]{0,2,1:T(8,128)(2,1)S(1)}, bf16[1536,2,64]{0,2,1:T(8,128)(2,1)}, u32[]{:S(2)}) copy-start(bf16[1536,2,64]{0,2,1:T(8,128)(2,1)} %copy-done.4) | copy-start | bytes 1179652 | tf_op jit(solution)/shard_map/while
  333.4 4.8 %copy-start.3 = (bf16[24,128,256]{2,1,0:T(8,128)(2,1)S(1)}, bf16[24,128,256]{2,1,0:T(8,128)(2,1)}, u32[]{:S(2)}) copy-start(bf16[24,128,256]{2,1,0:T(8,128)(2,1)} %copy-done.2) | copy-start | bytes 4718596 | tf_op jit(solution)/shard_map/while
  338.2 6.9 %copy-start.2 = (bf16[24,128,256]{2,1,0:T(8,128)(2,1)}, bf16[24,128,256]{2,1,0:T(8,128)(2,1)S(1)}, u32[]{:S(2)}) copy-start(bf16[24,128,256]{2,1,0:T(8,128)(2,1)S(1)} %get-tuple-element.755) | copy-start | bytes 4718596 | tf_op jit(solution)/shard_map/while
  345.9 2.1 copy-start.4
  356.9 4.7 %copy-start.5 = (bf16[1536,2,64]{0,2,1:T(8,128)(2,1)S(1)}, bf16[1536,2,64]{0,2,1:T(8,128)(2,1)}, u32[]{:S(2)}) copy-start(bf16[1536,2,64]{0,2,1:T(8,128)(2,1)} %copy-done.4) | copy-start | bytes 1179652 | tf_op jit(solution)/shard_map/while
  356.9 5.1 %copy-start.3 = (bf16[24,128,256]{2,1,0:T(8,128)(2,1)S(1)}, bf16[24,128,256]{2,1,0:T(8,128)(2,1)}, u32[]{:S(2)}) copy-start(bf16[24,128,256]{2,1,0:T(8,128)(2,1)} %copy-done.2) | copy-start | bytes 4718596 | tf_op jit(solution)/shard_map/while
  365.0 18.0 %collective-permute-start.2 = (f32[8,128,256]{2,1,0:T(8,128)}, f32[8,128,256]{2,1,0:T(8,128)S(1)}, u32[]{:S(2)}, u32[]{:S(2)}) collective-permute-start(f32[8,128,256]{2,1,0:T(8,128)} %get-tuple-element.505), channel_id=1, source_target_pairs={{8,0},{16,8},{24,16},{32,24},{40,32},{48,40},{56,48},{64,56},{72,6... | collective-permute-start | bytes 3145736 | tf_op jit(solution)/shard_map/ppermute | solution.py:30
  370.5 18.4 %collective-permute-start.3 = (f32[8,128,256]{2,1,0:T(8,128)}, f32[8,128,256]{2,1,0:T(8,128)S(1)}, u32[]{:S(2)}, u32[]{:S(2)}) collective-permute-start(f32[8,128,256]{2,1,0:T(8,128)} %get-tuple-element.506), channel_id=1, source_target_pairs={{0,8},{8,16},{16,24},{24,32},{32,40},{40,48},{48,56},{56,64},{64,7... | collective-permute-start | bytes 3145736 | tf_op jit(solution)/shard_map/ppermute | solution.py:30
  391.2 12.6 %copy-start.1 = (bf16[128,1024]{1,0:T(8,128)(2,1)S(1)}, bf16[128,1024]{1,0:T(8,128)(2,1)}, u32[]{:S(2)}) copy-start(bf16[128,1024]{1,0:T(8,128)(2,1)} %param.15) | copy-start | bytes 786436
  (3 other events, 4.9 us)
Sparse Core Ops, SparseCore 0:
  22.0 46.8 all-gather.3
  166.5 145.0 all-gather.5
